TPU v7x, 32 devices: a whole 2x2x4 slice. The times are simulated.
32 devices in a mesh: groups: 2 (over y), row: 4 (over z), col: 4 (over x, core).
Axes of the slice: x: 2, y: 2, z: 4, core: 2. Of those that a mesh axis runs over, the one named last changes fastest.
Arguments:
- right_side: float32 [128, 8192], P('groups', ('row', 'col')), parts along dimension 0, may hold values from -6 to 6
- prior: float32 [8192], P(('row', 'col')), may hold values from 0.5 to 2
- blocks: bfloat16 [1024, 128, 128], P(('row', 'col')), may hold values from -0.125 to 0.125
- block_row: int32 [1024], P(('row', 'col')), may hold values from 0 to 63, as said below
- block_col: int32 [1024], P(('row', 'col')), may hold values from 0 to 63, as said below
Outputs:
- solution_field: float32 [128, 8192], P('groups', ('row', 'col')), parts along dimension 0
- residual: float32 [128, 8192], P('groups', ('row', 'col')), parts along dimension 0
There are 2 independent parts, one for each index of `groups`. A program takes and returns all parts, laid end to end along the dimension named above; an argument that names none is the same for every part. Nothing has to cross between parts.
Inputs may be any that keep to these rules, and one draw needn't show every extreme that they name: `block_row`: stored blocks k*64 to (k+1)*64 - 1 belong to device k of row+col, k = r*4+c; their block rows lie in r*16 to (r+1)*16 - 1. `block_col`: the block columns b of device (r, c) satisfy (b // 4) % 4 == c.
All inputs are finite; a program needn't handle non-finite values.
Results may differ from a plain program's by a relative error of at most 0.0069.
Values may be sent and summed in bfloat16 or wider, within the bound.
A program may use at most 64 MiB of HBM per device.

v0:
```python
import jax
import jax.numpy as jnp
from jax import lax
from jax.sharding import PartitionSpec as P

BLOCK = 128
ITERS = 2


def spd_solve(matrix, rhs):
    factor = jnp.linalg.cholesky(matrix)
    half_solved = lax.linalg.triangular_solve(factor, rhs, left_side=True, lower=True)
    return lax.linalg.triangular_solve(
        factor, half_solved, left_side=True, lower=True, transpose_a=True
    )


def pair_gram(left, right):
    return lax.dot_general(
        left,
        right,
        (((1,), (1,)), ((), ())),
        precision=lax.Precision.HIGHEST,
        preferred_element_type=jnp.float32,
    )


def apply_left(coeffs, panel):
    return jnp.dot(
        coeffs, panel, precision=lax.Precision.HIGHEST, preferred_element_type=jnp.float32
    )


def forward_part(blocks, col_local, row_onehot, search):
    frames = search.shape[0]
    panel_view = search.reshape(frames, -1, BLOCK)
    picked = jnp.take(panel_view, col_local, axis=1)
    contrib = jnp.einsum("fkj,kij->fki", picked, blocks, preferred_element_type=jnp.float32)
    summed = jnp.einsum("rk,fki->fri", row_onehot, contrib, precision=lax.Precision.HIGHEST)
    return summed.reshape(frames, -1)


def backward_part(blocks, row_local, col_onehot, footprint):
    frames = footprint.shape[0]
    foot_view = footprint.reshape(frames, -1, BLOCK)
    picked = jnp.take(foot_view, row_local, axis=1)
    contrib = jnp.einsum("fki,kij->fkj", picked, blocks, preferred_element_type=jnp.float32)
    summed = jnp.einsum("ck,fkj->fcj", col_onehot, contrib, precision=lax.Precision.HIGHEST)
    return summed.reshape(frames, -1)


def shards(right_side, prior, blocks, block_row, block_col):
    pix_dev = right_side.shape[1]
    stretch_blocks = pix_dev // BLOCK
    rows_axis = lax.axis_size("row")
    cols_axis = lax.axis_size("col")
    row_span = stretch_blocks * cols_axis
    row_local = block_row % row_span
    col_local = block_col // row_span * stretch_blocks + block_col % stretch_blocks
    row_onehot = (jnp.arange(row_span, dtype=jnp.int32)[:, None] == row_local[None, :]).astype(
        jnp.float32
    )
    col_onehot = (
        jnp.arange(stretch_blocks * rows_axis, dtype=jnp.int32)[:, None] == col_local[None, :]
    ).astype(jnp.float32)
    solution = jnp.zeros_like(right_side)
    residual = right_side
    direction = right_side
    gram = lax.psum(pair_gram(residual, residual), ("row", "col"))
    for iteration in range(ITERS):
        final_step = iteration + 1 == ITERS
        search = lax.all_gather(direction.astype(jnp.bfloat16), "row", axis=1, tiled=True)
        foot_part = forward_part(blocks, col_local, row_onehot, search)
        foot_own = lax.psum_scatter(foot_part, "col", scatter_dimension=1, tiled=True).astype(
            jnp.bfloat16
        )
        foot_rows = lax.all_gather(foot_own, "col", axis=1, tiled=True)
        image_part = backward_part(blocks, row_local, col_onehot, foot_rows)
        image = (
            lax.psum_scatter(image_part, "row", scatter_dimension=1, tiled=True)
            + prior[None, :] * direction
        )
        if not final_step:
            curvature, cross, image_gram = lax.psum(
                (pair_gram(direction, image), pair_gram(image, residual), pair_gram(image, image)),
                ("row", "col"),
            )
        else:
            curvature = lax.psum(pair_gram(direction, image), ("row", "col"))
        step_alpha = spd_solve(curvature, gram)
        solution = solution + apply_left(step_alpha.T, direction)
        new_residual = residual - apply_left(step_alpha.T, image)
        if not final_step:
            new_gram = (
                gram
                - apply_left(cross.T, step_alpha)
                - apply_left(step_alpha.T, cross)
                + apply_left(apply_left(step_alpha.T, image_gram), step_alpha)
            )
            step_beta = spd_solve(gram, new_gram)
            direction = new_residual + apply_left(step_beta.T, direction)
            gram = new_gram
        residual = new_residual
    return (solution, residual)


def solution(mesh):
    return jax.shard_map(
        shards,
        mesh=mesh,
        in_specs=(
            P("groups", ("row", "col")),
            P(("row", "col")),
            P(("row", "col"), None, None),
            P(("row", "col")),
            P(("row", "col")),
        ),
        out_specs=(P("groups", ("row", "col")), P("groups", ("row", "col"))),
        check_vma=False,
    )
```

profile of v0, /device:TPU:0, one launch (start us, length us, event | category | flops | bytes accessed | tf_op | source)
XLA Modules:
  0.0 369.7 jit_solution(2030040030827632624)
XLA Ops:
  9.0 15.7 %all_gather.12 = bf16[64,2048]{1,0:T(8,128)(2,1)S(1)} all-gather(bf16[64,512]{1,0:T(8,128)(2,1)S(1)} %convert_element_type.14), channel_id=1, replica_groups=mesh['groups'=2,'row'=4,'col'=4] {'row'}, dimensions={1}, use_global_device_ids=true | all-gather | bytes 327680 | tf_op jit(solution)/shard_map/all_gather | solution.py:72
  27.7 2.0 fusion.6
  30.7 23.3 %reduce-scatter.5.cloned.1.call-done = f32[64,512]{1,0:T(8,128)} async-done(((f32[64,2048]{1,0:T(8,128)}), f32[64,512]{1,0:T(8,128)}) %reduce-scatter.5.cloned.1.call-update) | async-done | bytes 131088 | tf_op jit(solution)/shard_map/reduce_scatter | solution.py:74
  54.9 5.8 %all_gather.13 = bf16[64,2048]{1,0:T(8,128)(2,1)S(1)} all-gather(bf16[64,512]{1,0:T(8,128)(2,1)S(1)} %convert_element_type.15), channel_id=1, replica_groups=mesh['groups'=2,'row'=4,'col'=4] {'col'}, dimensions={1}, use_global_device_ids=true | all-gather | bytes 327680 | tf_op jit(solution)/shard_map/all_gather | solution.py:77
  62.3 2.0 fusion.4
  66.2 21.1 %reduce-scatter.7.cloned.1.call-done = f32[64,512]{1,0:T(8,128)} async-done(((f32[64,2048]{1,0:T(8,128)}), f32[64,512]{1,0:T(8,128)}) %reduce-scatter.7.cloned.1.call-update) | async-done | bytes 131088 | tf_op jit(solution)/shard_map/reduce_scatter | solution.py:80
  87.2 1.9 fusion.26
  89.1 1.9 fusion.25
  91.2 87.5 %all-reduce.3.cloned.1.call-done = (f32[64,64]{0,1:T(8,128)}, f32[64,64]{0,1:T(8,128)}, f32[64,64]{1,0:T(8,128)}, f32[64,64]{1,0:T(8,128)}) async-done(((f32[64,64]{0,1:T(8,128)}, f32[64,64]{0,1:T(8,128)}, f32[64,64]{1,0:T(8,128)}, f32[64,64]{1,0:T(8,128)}), (f32[64,64]{0,1:T(8,128)}, f32[64,64]{0,1:T(8,128)}, f32[64,64]{1,0:T(8,128)}, f32[64,64]{1,0:T(8,128)})) %all-reduce.3.cloned.1.call-update) | async-done | bytes 65552 | tf_op jit(solution)/shard_map/psum | solution.py:69
  181.2 5.8 %cholesky.70 = f32[64,64]{1,0:T(8,128)S(1)} custom-call(f32[64,64]{1,0:T(8,128)S(1)} %get-tuple-element.16), custom_call_target="Cholesky" | custom-call | tf_op jit(solution)/shard_map/jit(cholesky)/cholesky | solution.py:11
  188.4 4.9 %custom-call.15 = f32[1,64,64]{1,2,0:T(8,128)S(1)} custom-call(f32[1,64,64]{2,1,0:T(8,128)S(1)} %fusion.33), custom_call_target="InvertDiagBlocksLowerTriangular" | custom-call | tf_op jit(solution)/shard_map/triangular_solve/custom-call.2 | solution.py:13
  193.3 5.9 %cholesky.59 = f32[64,64]{1,0:T(8,128)S(1)} custom-call(f32[64,64]{1,0:T(8,128)S(1)} %get-tuple-element.17), custom_call_target="Cholesky" | custom-call | tf_op jit(solution)/shard_map/jit(cholesky)/cholesky | solution.py:11
  200.5 4.9 %custom-call.13 = f32[1,64,64]{1,2,0:T(8,128)S(1)} custom-call(f32[1,64,64]{2,1,0:T(8,128)S(1)} %fusion.32), custom_call_target="InvertDiagBlocksLowerTriangular" | custom-call | tf_op jit(solution)/shard_map/triangular_solve/custom-call.2 | solution.py:13
  212.0 15.7 %all_gather.14 = bf16[64,2048]{1,0:T(8,128)(2,1)S(1)} all-gather(bf16[64,512]{1,0:T(8,128)(2,1)S(1)} %get-tuple-element.14), channel_id=1, replica_groups=mesh['groups'=2,'row'=4,'col'=4] {'row'}, dimensions={1}, use_global_device_ids=true | all-gather | bytes 327680 | tf_op jit(solution)/shard_map/all_gather | solution.py:72
  228.5 2.2 convolution_bitcast_fusion.1
  230.7 2.0 fusion.2
  233.6 21.8 %reduce-scatter.9.cloned.1.call-done = f32[64,512]{1,0:T(8,128)} async-done(((f32[64,2048]{1,0:T(8,128)}), f32[64,512]{1,0:T(8,128)}) %reduce-scatter.9.cloned.1.call-update) | async-done | bytes 131088 | tf_op jit(solution)/shard_map/reduce_scatter | solution.py:74
  256.3 6.0 %all_gather.15 = bf16[64,2048]{1,0:T(8,128)(2,1)S(1)} all-gather(bf16[64,512]{1,0:T(8,128)(2,1)S(1)} %convert_element_type.17), channel_id=1, replica_groups=mesh['groups'=2,'row'=4,'col'=4] {'col'}, dimensions={1}, use_global_device_ids=true | all-gather | bytes 327680 | tf_op jit(solution)/shard_map/all_gather | solution.py:77
  263.9 2.0 fusion
  267.2 21.7 %reduce-scatter.11.cloned.1.call-done = f32[64,512]{1,0:T(8,128)} async-done(((f32[64,2048]{1,0:T(8,128)}), f32[64,512]{1,0:T(8,128)}) %reduce-scatter.11.cloned.1.call-update) | async-done | bytes 131088 | tf_op jit(solution)/shard_map/reduce_scatter | solution.py:80
  290.1 57.6 %psum.39 = f32[64,64]{0,1:T(8,128)S(1)} all-reduce(f32[64,64]{0,1:T(8,128)S(1)} %fusion.24), channel_id=1, replica_groups=mesh['groups'=2,'row'=4,'col'=4] {'row','col'}, use_global_device_ids=true, to_apply=%region_10.15 | all-reduce | flops 4096 | bytes 32768 | tf_op jit(solution)/shard_map/psum | solution.py:89
  347.8 5.8 %cholesky.81 = f32[64,64]{1,0:T(8,128)S(1)} custom-call(f32[64,64]{1,0:T(8,128)S(1)} %fusion.39), custom_call_target="Cholesky" | custom-call | tf_op jit(solution)/shard_map/jit(cholesky)/cholesky | solution.py:11
  355.0 4.9 %custom-call.17 = f32[1,64,64]{1,2,0:T(8,128)S(1)} custom-call(f32[1,64,64]{2,1,0:T(8,128)S(1)} %fusion.34), custom_call_target="InvertDiagBlocksLowerTriangular" | custom-call | tf_op jit(solution)/shard_map/triangular_solve/custom-call.2 | solution.py:13
  361.3 1.9 convolution_subtract_fusion
  (96 shorter events, 31.5 us)
Async XLA Ops:
  7.2 19.0 %copy-start = (bf16[64,128,128]{2,1,0:T(8,128)(2,1)S(1)}, bf16[64,128,128]{2,1,0:T(8,128)(2,1)}, u32[]{:S(2)}) copy-start(bf16[64,128,128]{2,1,0:T(8,128)(2,1)} %param.14) | copy-start | bytes 6291460
  7.2 46.8 %reduce-scatter.5.cloned.1.call-start = ((), (), s32[]{:S(2)}) async-start(), calls=%async_computation.4 | async-start | bytes 655360 | tf_op jit(solution)/shard_map/reduce_scatter | solution.py:74
  8.0 19.7 %copy-start.15 = (pred[64]{0:T(512)(128)(4,1)}, pred[64]{0:T(512)(128)(4,1)S(1)}, u32[]{:S(2)}) copy-start(pred[64]{0:T(512)(128)(4,1)S(1)} %get-tuple-element.12) | copy-start | bytes 196
  25.4 5.3 %copy-start.11 = (s32[64]{0:T(128)}, s32[64]{0:T(128)S(1)}, u32[]{:S(2)}) copy-start(s32[64]{0:T(128)S(1)} %get-tuple-element.11) | copy-start | bytes 772
  25.4 36.1 %copy-start.13 = (pred[64]{0:T(512)(128)(4,1)}, pred[64]{0:T(512)(128)(4,1)S(1)}, u32[]{:S(2)}) copy-start(pred[64]{0:T(512)(128)(4,1)S(1)} %get-tuple-element.10) | copy-start | bytes 196
  30.7 56.6 %reduce-scatter.7.cloned.1.call-start = ((), (), s32[]{:S(2)}) async-start(), calls=%async_computation.5 | async-start | bytes 655360 | tf_op jit(solution)/shard_map/reduce_scatter | solution.py:80
  62.3 3.0 copy-start.1
  62.3 25.0 %copy-start.10 = (f32[512]{0:T(512)S(1)}, f32[512]{0:T(512)}, u32[]{:S(2)}) copy-start(f32[512]{0:T(512)} %param.13) | copy-start | bytes 6148
  65.2 113.5 %all-reduce.3.cloned.1.call-start = ((), (), s32[]{:S(2)}) async-start(), calls=%async_computation.8 | async-start | bytes 262144 | tf_op jit(solution)/shard_map/psum | solution.py:69
  87.2 123.4 %copy-start.5 = (f32[64,512]{1,0:T(8,128)S(1)}, f32[64,512]{1,0:T(8,128)}, u32[]{:S(2)}) copy-start(f32[64,512]{1,0:T(8,128)} %reduce-scatter.7.cloned.1.call-done) | copy-start | bytes 393220
  91.0 164.4 %reduce-scatter.9.cloned.1.call-start = ((), (), s32[]{:S(2)}) async-start(), calls=%async_computation.6 | async-start | bytes 655360 | tf_op jit(solution)/shard_map/reduce_scatter | solution.py:74
  206.6 21.1 %copy-start.3 = (f32[64,64]{1,0:T(8,128)}, f32[64,64]{1,0:T(8,128)S(1)}, u32[]{:S(2)}) copy-start(f32[64,64]{1,0:T(8,128)S(1)} %fusion.47) | copy-start | bytes 49156
  209.9 0.6 copy-start.8
  211.0 16.7 %copy-start.6 = (f32[64,512]{1,0:T(8,128)}, f32[64,512]{1,0:T(8,128)S(1)}, u32[]{:S(2)}) copy-start(f32[64,512]{1,0:T(8,128)S(1)} %convolution_subtract_fusion.1) | copy-start | bytes 393220
  228.5 2.2 copy-start.12
  233.6 29.6 %copy-start.14 = (pred[64]{0:T(512)(128)(4,1)S(1)}, pred[64]{0:T(512)(128)(4,1)}, u32[]{:S(2)}) copy-start(pred[64]{0:T(512)(128)(4,1)} %copy-done.13) | copy-start | bytes 196
  233.6 55.3 %reduce-scatter.11.cloned.1.call-start = ((), (), s32[]{:S(2)}) async-start(), calls=%async_computation.7 | async-start | bytes 655360 | tf_op jit(solution)/shard_map/reduce_scatter | solution.py:80
  263.9 3.0 copy-start.4
  263.9 25.0 %copy-start.2 = (f32[64,512]{1,0:T(8,128)S(1)}, f32[64,512]{1,0:T(8,128)}, u32[]{:S(2)}) copy-start(f32[64,512]{1,0:T(8,128)} %get-tuple-element.15) | copy-start | bytes 393220
  263.9 96.0 %copy-start.9 = (f32[64,64]{0,1:T(8,128)S(1)}, f32[64,64]{0,1:T(8,128)}, u32[]{:S(2)}) copy-start(f32[64,64]{0,1:T(8,128)} %copy-done.8) | copy-start | bytes 49156
  265.9 95.4 %copy-start.7 = (f32[64,512]{1,0:T(8,128)S(1)}, f32[64,512]{1,0:T(8,128)}, u32[]{:S(2)}) copy-start(f32[64,512]{1,0:T(8,128)} %copy-done.6) | copy-start | bytes 393220
Sparse Core Ops, SparseCore 0:
  30.8 23.1 reduce-scatter.4
  65.4 21.8 reduce-scatter.6
  91.7 87.0 all-reduce.2
  233.7 21.6 reduce-scatter.8
  267.0 21.8 reduce-scatter.10
where the time goes:
time: 371 us; the launch traced here: 370 us
  waiting for transfers between devices  175 us (47%)
  blocking collectives  101 us (27%)
  other arithmetic  41.3 us (11%)
  matrix products  28.5 us (8%)
  between operations  14.3 us (4%)
  local copies, waits for them, and re-layouts  9.18 us (2%)
    psum x1, waiting for transfers between devices, shards(): gram = lax.psum(pair_gram(residual, residual), ('row', 'col'))  87.5 us
    psum x1, blocking collectives, shards(): curvature = lax.psum(pair_gram(direction, image), ('row', 'col'))  57.6 us
    reduce_scatter x2, waiting for transfers between devices, shards(): lax.psum_scatter(foot_part, 'col', scatter_dimension=1, tiled=True)  45 us
    reduce_scatter x2, waiting for transfers between devices, shards(): lax.psum_scatter(image_part, 'row', scatter_dimension=1, tiled=True)  42.8 us
    all_gather x2, blocking collectives, shards(): lax.all_gather(direction.astype(jnp.bfloat16), 'row', axis=1, tiled=True)  31.3 us
    another operation x9, other arithmetic, spd_solve(): factor = jnp.linalg.cholesky(matrix)  19.6 us
    another operation x6, other arithmetic, spd_solve(): lax.linalg.triangular_solve(factor, half_solved, left_side=True, lower=Tr...  16.6 us
    all_gather x2, blocking collectives, shards(): foot_rows = lax.all_gather(foot_own, 'col', axis=1, tiled=True)  11.8 us
  transfers between devices with their start and end apart: 5, of which 5 were waited for; matrix products, arithmetic and copies ran while one was open for 0% of the time, Pallas kernels for 0%

commit v1 on v0

v1 whole, which is shorter than its diff:
```python
import functools

import jax
import jax.numpy as jnp
from jax import lax
from jax.experimental import pallas as pl
from jax.experimental.pallas import tpu as pltpu
from jax.sharding import PartitionSpec as P

BLOCK = 128
ITERS = 2
UNROLL = 8
MESH = pl.DeviceIdType.MESH
HIGHEST = lax.Precision.HIGHEST
f32 = jnp.float32
bf16 = jnp.bfloat16


def dot(left, right, dims):
    return lax.dot_general(
        left, right, (dims, ((), ())), precision=HIGHEST, preferred_element_type=f32
    )


def pair_gram(left, right):
    return dot(left, right, ((1,), (1,)))


def left_t(coeffs, panel):
    return dot(coeffs, panel, ((0,), (0,)))


def gauss_jordan(aug, frames):
    rows = lax.broadcasted_iota(jnp.int32, aug.shape, 0)
    for j in range(frames):
        at = frames + j
        lead = aug[j : j + 1, :] * (1.0 / aug[j : j + 1, at : at + 1])
        aug = jnp.where(rows == j, lead, aug - aug[:, at : at + 1] * lead)
    return aug[:, :frames]


def kernel(
    nr, nc, cb, kb, frames,
    tab, keep, rhs_ref, prior_ref, blocks_hbm, sol_ref, res_ref,
    blocks, panel, foot, sendf, sendb, landf, landb, scan, image, direct, aug,
    gc0, gr0, gc1, gr1, gc2, gr2,
    blk_sem, ag_s, ag_r, rs_s, rs_r, fg_s, fg_r, br_s, br_r, gc_s, gc_r, gr_s, gr_r,
):
    r = lax.axis_index("row")
    c = lax.axis_index("col")
    nrow, ncol = cb * nc, cb * nr
    half = frames // 2
    pending = []

    load = pltpu.make_async_copy(blocks_hbm, blocks, blk_sem)
    load.start()

    barrier = pltpu.get_barrier_semaphore()
    for axis, me, n in (("row", r, nr), ("col", c, nc)):
        for o in range(1, n):
            pl.semaphore_signal(
                barrier, inc=1, device_id={axis: lax.rem(me + o, n)}, device_id_type=MESH
            )

    def send(axis, me, n, src, dst, ssem, rsem):
        copies = []
        for o in range(1, n):
            peer = lax.rem(me + o, n)
            copy = pltpu.make_async_remote_copy(
                src_ref=src(peer), dst_ref=dst(o), send_sem=ssem.at[o - 1],
                recv_sem=rsem.at[o - 1], device_id={axis: peer}, device_id_type=MESH,
            )
            copy.start()
            copies.append(copy)
        pending.extend(copies)
        return copies

    def arrive(copies):
        for copy in copies:
            copy.wait_recv()

    def share(axis, me, n, buf, ssem, rsem, width=1):
        at = lambda _: buf.at[pl.ds(me * width, width)]
        return send(axis, me, n, at, at, ssem, rsem)

    def total(buf, n):
        out = buf[0]
        for i in range(1, n):
            out = out + buf[i]
        return out

    def fold(buf, me, gram):
        buf[me, :, :frames] = gram[:half]
        buf[me, :, frames:] = gram[half:]

    def unfold(packed):
        return jnp.concatenate([packed[:, :frames], packed[:, frames:]], axis=0)

    def put_panel(it, value):
        for b in range(cb):
            panel[it, r * cb + b] = value[:, b * BLOCK : (b + 1) * BLOCK].astype(bf16)

    def gather_rows(it):
        return share("row", r, nr, panel.at[it], ag_s.at[it], ag_r.at[it], cb)

    def sweep(source, it, order_at, keep_at, side):
        def body(q, run):
            for u in range(UNROLL):
                t = q * UNROLL + u
                run = run * keep[keep_at + t] + lax.dot_general(
                    source[it, tab[order_at + kb + t]],
                    blocks[tab[order_at + t]],
                    (((1,), (side,)), ((), ())),
                    preferred_element_type=f32,
                )
                scan[t] = run
            return run

        lax.fori_loop(0, kb // UNROLL, body, jnp.zeros((frames, BLOCK), f32))

    def segment(end_at, valid_at, i):
        return scan[tab[end_at + i]] * keep[valid_at + i]

    tab_c = 2 * kb + nrow
    keep_c = kb + nrow

    rhs = rhs_ref[...]
    put_panel(0, rhs)
    fold(gc0, c, pair_gram(rhs, rhs))
    pl.semaphore_wait(barrier, nr + nc - 2)

    gather = gather_rows(0)
    gram_cols = share("col", c, nc, gc0, gc_s.at[0], gc_r.at[0])
    residual = rhs_ref
    gram = None
    for it in range(ITERS):
        last = it + 1 == ITERS
        now = rhs_ref if it == 0 else direct
        if it == 0:
            load.wait()
        arrive(gather)
        sweep(panel, it, 0, 0, 1)
        for i in range(nrow):
            sendf[it, i] = segment(2 * kb, kb, i).astype(bf16)
        copies = send(
            "col", c, nc,
            lambda p: sendf.at[it, pl.ds(p * cb, cb)], lambda o: landf.at[it, o - 1],
            rs_s.at[it], rs_r.at[it],
        )
        if it == 0:
            arrive(gram_cols)
            gr0[r] = total(gc0, nc)
            gram_rows = share("row", r, nr, gr0, gr_s.at[0], gr_r.at[0])
        arrive(copies)
        for b in range(cb):
            own = segment(2 * kb, kb, c * cb + b)
            for o in range(1, nc):
                own = own + landf[it, o - 1, b].astype(f32)
            foot[it, c * cb + b] = own.astype(bf16)
        copies = share("col", c, nc, foot.at[it], fg_s.at[it], fg_r.at[it], cb)
        if it == 0:
            arrive(gram_rows)
            gram = unfold(total(gr0, nr))
            aug[:, frames:] = gram
            eye = lax.broadcasted_iota(jnp.int32, (frames, frames), 0)
            aug[:, :frames] = (
                eye == lax.broadcasted_iota(jnp.int32, (frames, frames), 1)
            ).astype(f32)
            gram_inverse = gauss_jordan(aug[...], frames)
        arrive(copies)
        sweep(foot, it, tab_c, keep_c, 0)
        for i in range(ncol):
            sendb[it, i] = segment(tab_c + 2 * kb, keep_c + kb, i).astype(bf16)
        copies = send(
            "row", r, nr,
            lambda p: sendb.at[it, pl.ds(p * cb, cb)], lambda o: landb.at[it, o - 1],
            br_s.at[it], br_r.at[it],
        )
        arrive(copies)
        for b in range(cb):
            at = slice(b * BLOCK, (b + 1) * BLOCK)
            own = segment(tab_c + 2 * kb, keep_c + kb, r * cb + b)
            for o in range(1, nr):
                own = own + landb[it, o - 1, b].astype(f32)
            image[:, at] = own + prior_ref[:, at] * now[:, at]
        direction = now[...]
        im = image[...]
        curvature = pair_gram(direction, im)
        if last:
            fold(gc2, c, curvature)
            cols, rows = gc2, gr2
        else:
            gc1[c, :, :frames] = curvature
            gc1[c, :, frames:] = pair_gram(im, im)
            cols, rows = gc1, gr1
        arrive(share("col", c, nc, cols, gc_s.at[it + 1], gc_r.at[it + 1]))
        rows[r] = total(cols, nc)
        arrive(share("row", r, nr, rows, gr_s.at[it + 1], gr_r.at[it + 1]))
        summed = total(rows, nr)
        curvature = unfold(summed) if last else summed[:, :frames]
        aug[:, :frames] = gram
        aug[:, frames:] = curvature
        alpha = gauss_jordan(aug[...], frames)
        new_residual = (rhs_ref if it == 0 else res_ref)[...] - left_t(alpha, im)
        res_ref[...] = new_residual
        if not last:
            image_gram = summed[:, frames:]
            mixed = dot(curvature, alpha, ((1,), (0,)))
            new_gram = (
                gram
                - mixed
                - left_t(alpha, curvature.T)
                + left_t(alpha, dot(image_gram, alpha, ((1,), (0,))))
            )
            beta = dot(gram_inverse, new_gram, ((1,), (0,)))
            direct[...] = new_residual + left_t(beta, direction)
            put_panel(it + 1, direct)
            gather = gather_rows(it + 1)
            gram = new_gram
        update = left_t(alpha, direction)
        sol_ref[...] = update if it == 0 else sol_ref[...] + update
    for copy in pending:
        copy.wait_send()


def order_by(key, other, count):
    kb = key.shape[0]
    ids = jnp.arange(kb, dtype=jnp.int32)
    full = key * kb + ids
    rank = jnp.sum((full[None, :] < full[:, None]).astype(jnp.int32), axis=1)
    onehot = (rank[None, :] == ids[:, None]).astype(jnp.int32)
    order = jnp.sum(onehot * ids[None, :], axis=1)
    picks = jnp.sum(onehot * other[None, :], axis=1)
    keys = jnp.sum(onehot * key[None, :], axis=1)
    keep = jnp.concatenate([jnp.zeros((1,), f32), (keys[1:] == keys[:-1]).astype(f32)])
    slots = jnp.arange(count, dtype=jnp.int32)[:, None]
    ends = jnp.maximum(jnp.sum((key[None, :] <= slots).astype(jnp.int32), axis=1) - 1, 0)
    valid = jnp.max((key[None, :] == slots).astype(f32), axis=1)
    return [order, picks, ends], [keep, valid]


def shards(right_side, prior, blocks, block_row, block_col):
    frames, pix = right_side.shape
    kb = blocks.shape[0]
    cb = pix // BLOCK
    nr = lax.axis_size("row")
    nc = lax.axis_size("col")
    nrow, ncol = cb * nc, cb * nr
    row_local = block_row % nrow
    col_local = block_col // nrow * cb + block_col % cb
    ints_r, keep_r = order_by(row_local, col_local, nrow)
    ints_c, keep_c = order_by(col_local, row_local, ncol)
    tab = jnp.concatenate(ints_r + ints_c)
    keep = jnp.concatenate(keep_r + keep_c)
    vm = pl.BlockSpec(memory_space=pltpu.VMEM)
    sm = pl.BlockSpec(memory_space=pltpu.SMEM)
    dma = pltpu.SemaphoreType.DMA
    tile = (frames, BLOCK)
    half = (frames // 2, 2 * frames)
    wide = (frames, 2 * frames)
    out = jax.ShapeDtypeStruct(right_side.shape, f32)
    return pl.pallas_call(
        functools.partial(kernel, nr, nc, cb, kb, frames),
        out_shape=(out, out),
        in_specs=[sm, sm, vm, vm, pl.BlockSpec(memory_space=pl.ANY)],
        out_specs=(vm, vm),
        scratch_shapes=[
            pltpu.VMEM(blocks.shape, bf16),
            pltpu.VMEM((ITERS, ncol) + tile, bf16),
            pltpu.VMEM((ITERS, nrow) + tile, bf16),
            pltpu.VMEM((ITERS, nrow) + tile, bf16),
            pltpu.VMEM((ITERS, ncol) + tile, bf16),
            pltpu.VMEM((ITERS, nc - 1, cb) + tile, bf16),
            pltpu.VMEM((ITERS, nr - 1, cb) + tile, bf16),
            pltpu.VMEM((kb,) + tile, f32),
            pltpu.VMEM(right_side.shape, f32),
            pltpu.VMEM(right_side.shape, f32),
            pltpu.VMEM(wide, f32),
            pltpu.VMEM((nc,) + half, f32),
            pltpu.VMEM((nr,) + half, f32),
            pltpu.VMEM((nc,) + wide, f32),
            pltpu.VMEM((nr,) + wide, f32),
            pltpu.VMEM((nc,) + half, f32),
            pltpu.VMEM((nr,) + half, f32),
            dma,
            dma((ITERS, nr - 1)), dma((ITERS, nr - 1)),
            dma((ITERS, nc - 1)), dma((ITERS, nc - 1)),
            dma((ITERS, nc - 1)), dma((ITERS, nc - 1)),
            dma((ITERS, nr - 1)), dma((ITERS, nr - 1)),
            dma((ITERS + 1, nc - 1)), dma((ITERS + 1, nc - 1)),
            dma((ITERS + 1, nr - 1)), dma((ITERS + 1, nr - 1)),
        ],
        compiler_params=pltpu.CompilerParams(
            collective_id=0, has_side_effects=True, vmem_limit_bytes=48 << 20
        ),
    )(tab, keep, right_side, prior[None, :], blocks)


def solution(mesh):
    return jax.shard_map(
        shards,
        mesh=mesh,
        in_specs=(
            P("groups", ("row", "col")),
            P(("row", "col")),
            P(("row", "col"), None, None),
            P(("row", "col")),
            P(("row", "col")),
        ),
        out_specs=(P("groups", ("row", "col")), P("groups", ("row", "col"))),
        check_vma=False,
    )
```

time: 371 us -> 95.7 us (0.26)
  waiting for transfers between devices: 175 us -> 0 us
  blocking collectives: 101 us -> 0 us
  Pallas kernels: 0 us -> 87.8 us
  other arithmetic: 41.3 us -> 2.3 us
  matrix products: 28.5 us -> 0 us
  between operations: 14.3 us -> 0.66 us
  local copies, waits for them, and re-layouts: 9.18 us -> 4.66 us
    pallas_call x0 -> x1, Pallas kernels: none -> 87.8 us  [shards(): pl.pallas_call(functools.partial(kernel, nr, nc, cb, kb, frames), out_sha...]
    reduce_scatter x4 -> x0, waiting for transfers between devices: 87.8 us -> none  [the longest x2 45 us: shards(): lax.psum_scatter(foot_part, 'col', scatter_dimension=1, tiled=True)]
    psum x1 -> x0, waiting for transfers between devices: 87.5 us -> none  [shards(): gram = lax.psum(pair_gram(residual, residual), ('row', 'col'))]
    psum x1 -> x0, blocking collectives: 57.6 us -> none  [shards(): curvature = lax.psum(pair_gram(direction, image), ('row', 'col'))]
    all_gather x4 -> x0, blocking collectives: 43.1 us -> none  [the longest x2 31.3 us: shards(): lax.all_gather(direction.astype(jnp.bfloat16), 'row', axis=1, tiled=True)]
    another operation x15 -> x0, other arithmetic: 36.2 us -> none  [the longest x9 19.6 us: spd_solve(): factor = jnp.linalg.cholesky(matrix)]
    dot_general x21 -> x0, matrix products: 26.5 us -> none  [the longest x9 7.73 us: apply_left(): jnp.dot(coeffs, panel, precision=lax.Precision.HIGHEST, preferred_element...]
  transfers between devices with their start and end apart: 5 -> 0, of which waited for: 5 -> 0; matrix products, arithmetic and copies ran while one was open for 0% -> 0% of each run, Pallas kernels for 0% -> 0%
where the time goes in v1:
time: 95.7 us; the launch traced here: 95.5 us
  Pallas kernels  87.8 us (92%)
  local copies, waits for them, and re-layouts  4.66 us (5%)
  other arithmetic  2.3 us (2%)
    pallas_call x1, Pallas kernels, shards(): pl.pallas_call(functools.partial(kernel, nr, nc, cb, kb, frames), out_sha...  87.8 us
    unnamed x8, local copies, waits for them, and re-layouts  4.5 us

profile of v1, /device:TPU:0, one launch (start us, length us, event | category | flops | bytes accessed | tf_op | source)
XLA Modules:
  0.0 95.5 jit_solution(5768606446794198207)
XLA Ops:
  0.6 0.7 iota_add_fusion.1
  1.3 0.2 convert_reduce_fusion.1
  1.5 0.1 convert_reduce_fusion.5
  1.6 0.7 iota_add_fusion
  2.3 0.2 convert_reduce_fusion
  2.4 0.1 convert_reduce_fusion.4
  2.6 0.1 convert_reduce_fusion.2
  2.7 0.2 select_reduce_fusion
  2.9 0.1 compare_convert_fusion
  3.0 0.1 concatenate.7.keep
  3.0 0.1 concatenate.6.tab
  3.1 0.0 copy-start
  3.1 1.6 %copy-done = bf16[64,128,128]{2,1,0:T(8,128)(2,1)S(1)} copy-done((bf16[64,128,128]{2,1,0:T(8,128)(2,1)S(1)}, bf16[64,128,128]{2,1,0:T(8,128)(2,1)}, u32[]{:S(2)}) %copy-start) | copy-done | bytes 2097176
  4.7 0.0 copy-start.1
  4.7 0.9 copy-done.1
  5.6 0.0 copy-start.2
  5.6 0.7 copy-done.2
  6.3 87.8 %shard_map.68 = (f32[64,512]{1,0:T(8,128)S(1)}, f32[64,512]{1,0:T(8,128)S(1)}) custom-call(s32[288]{0:T(512)S(1)} %concatenate.6.tab, f32[160]{0:T(256)S(1)} %concatenate.7.keep, f32[64,512]{1,0:T(8,128)S(1)} %copy-done.1, f32[1,512]{1,0:T(1,128)S(1)} %bitcast.1, bf16[64,128,128]{2,1,0:T(8,128)(2,1)S(1)} %copy-done), custom_call_target="tpu_custom_call" | custom-call | tf_op jit(solution)/shard_map/pallas_call | solution.py:262
  94.2 0.7 copy.9
  94.8 0.7 copy.10
  (1 shorter events, 0.0 us)
Async XLA Ops:
  3.1 1.6 %copy-start = (bf16[64,128,128]{2,1,0:T(8,128)(2,1)S(1)}, bf16[64,128,128]{2,1,0:T(8,128)(2,1)}, u32[]{:S(2)}) copy-start(bf16[64,128,128]{2,1,0:T(8,128)(2,1)} %blocks_hbm.1) | copy-start | bytes 6291460
  4.7 0.9 copy-start.1
  5.6 0.7 copy-start.2

commit v2 on v1

--- a/solution.py
+++ b/solution.py
@@ -45,6 +45,7 @@
     blocks, panel, foot, sendf, sendb, landf, landb, scan, image, direct, aug,
     gc0, gr0, gc1, gr1, gc2, gr2,
     blk_sem, ag_s, ag_r, rs_s, rs_r, fg_s, fg_r, br_s, br_r, gc_s, gc_r, gr_s, gr_r,
+    nc_s, nc_r, nr_s, nr_r,
 ):
     r = lax.axis_index("row")
     c = lax.axis_index("col")
@@ -131,7 +132,6 @@
 
     gather = gather_rows(0)
     gram_cols = share("col", c, nc, gc0, gc_s.at[0], gc_r.at[0])
-    residual = rhs_ref
     gram = None
     for it in range(ITERS):
         last = it + 1 == ITERS
@@ -151,13 +151,21 @@
             arrive(gram_cols)
             gr0[r] = total(gc0, nc)
             gram_rows = share("row", r, nr, gr0, gr_s.at[0], gr_r.at[0])
+        direction = now[...]
+        curvature = pair_gram(direction, prior_ref[...] * direction)
         arrive(copies)
         for b in range(cb):
             own = segment(2 * kb, kb, c * cb + b)
             for o in range(1, nc):
                 own = own + landf[it, o - 1, b].astype(f32)
-            foot[it, c * cb + b] = own.astype(bf16)
+            rounded = own.astype(bf16)
+            foot[it, c * cb + b] = rounded
+            image[:, b * BLOCK : (b + 1) * BLOCK] = own
         copies = share("col", c, nc, foot.at[it], fg_s.at[it], fg_r.at[it], cb)
+        own = image[...]
+        curvature = curvature + pair_gram(own, own.astype(bf16).astype(f32))
+        fold(gc1.at[it], c, curvature)
+        curve_cols = share("col", c, nc, gc1.at[it], gc_s.at[it + 1], gc_r.at[it + 1])
         if it == 0:
             arrive(gram_rows)
             gram = unfold(total(gr0, nr))
@@ -167,6 +175,9 @@
                 eye == lax.broadcasted_iota(jnp.int32, (frames, frames), 1)
             ).astype(f32)
             gram_inverse = gauss_jordan(aug[...], frames)
+        arrive(curve_cols)
+        gr1[it, r] = total(gc1.at[it], nc)
+        curve_rows = share("row", r, nr, gr1.at[it], gr_s.at[it + 1], gr_r.at[it + 1])
         arrive(copies)
         sweep(foot, it, tab_c, keep_c, 0)
         for i in range(ncol):
@@ -176,6 +187,13 @@
             lambda p: sendb.at[it, pl.ds(p * cb, cb)], lambda o: landb.at[it, o - 1],
             br_s.at[it], br_r.at[it],
         )
+        arrive(curve_rows)
+        curvature = unfold(total(gr1.at[it], nr))
+        aug[:, :frames] = gram
+        aug[:, frames:] = 0.5 * (curvature + curvature.T)
+        alpha = gauss_jordan(aug[...], frames)
+        update = left_t(alpha, direction)
+        sol_ref[...] = update if it == 0 else sol_ref[...] + update
         arrive(copies)
         for b in range(cb):
             at = slice(b * BLOCK, (b + 1) * BLOCK)
@@ -183,42 +201,18 @@
             for o in range(1, nr):
                 own = own + landb[it, o - 1, b].astype(f32)
             image[:, at] = own + prior_ref[:, at] * now[:, at]
-        direction = now[...]
-        im = image[...]
-        curvature = pair_gram(direction, im)
-        if last:
-            fold(gc2, c, curvature)
-            cols, rows = gc2, gr2
-        else:
-            gc1[c, :, :frames] = curvature
-            gc1[c, :, frames:] = pair_gram(im, im)
-            cols, rows = gc1, gr1
-        arrive(share("col", c, nc, cols, gc_s.at[it + 1], gc_r.at[it + 1]))
-        rows[r] = total(cols, nc)
-        arrive(share("row", r, nr, rows, gr_s.at[it + 1], gr_r.at[it + 1]))
-        summed = total(rows, nr)
-        curvature = unfold(summed) if last else summed[:, :frames]
-        aug[:, :frames] = gram
-        aug[:, frames:] = curvature
-        alpha = gauss_jordan(aug[...], frames)
-        new_residual = (rhs_ref if it == 0 else res_ref)[...] - left_t(alpha, im)
-        res_ref[...] = new_residual
+        residual = (rhs_ref if it == 0 else res_ref)[...] - left_t(alpha, image[...])
+        res_ref[...] = residual
         if not last:
-            image_gram = summed[:, frames:]
-            mixed = dot(curvature, alpha, ((1,), (0,)))
-            new_gram = (
-                gram
-                - mixed
-                - left_t(alpha, curvature.T)
-                + left_t(alpha, dot(image_gram, alpha, ((1,), (0,))))
-            )
-            beta = dot(gram_inverse, new_gram, ((1,), (0,)))
-            direct[...] = new_residual + left_t(beta, direction)
+            fold(gc2.at[it], c, pair_gram(residual, residual))
+            arrive(share("col", c, nc, gc2.at[it], nc_s.at[it], nc_r.at[it]))
+            gr2[it, r] = total(gc2.at[it], nc)
+            arrive(share("row", r, nr, gr2.at[it], nr_s.at[it], nr_r.at[it]))
+            gram = unfold(total(gr2.at[it], nr))
+            beta = dot(gram_inverse, gram, ((1,), (0,)))
+            direct[...] = residual + left_t(beta, direction)
             put_panel(it + 1, direct)
             gather = gather_rows(it + 1)
-            gram = new_gram
-        update = left_t(alpha, direction)
-        sol_ref[...] = update if it == 0 else sol_ref[...] + update
     for copy in pending:
         copy.wait_send()
 
@@ -278,10 +272,10 @@
             pltpu.VMEM(wide, f32),
             pltpu.VMEM((nc,) + half, f32),
             pltpu.VMEM((nr,) + half, f32),
-            pltpu.VMEM((nc,) + wide, f32),
-            pltpu.VMEM((nr,) + wide, f32),
-            pltpu.VMEM((nc,) + half, f32),
-            pltpu.VMEM((nr,) + half, f32),
+            pltpu.VMEM((ITERS, nc) + half, f32),
+            pltpu.VMEM((ITERS, nr) + half, f32),
+            pltpu.VMEM((ITERS - 1, nc) + half, f32),
+            pltpu.VMEM((ITERS - 1, nr) + half, f32),
             dma,
             dma((ITERS, nr - 1)), dma((ITERS, nr - 1)),
             dma((ITERS, nc - 1)), dma((ITERS, nc - 1)),
@@ -289,6 +283,8 @@
             dma((ITERS, nr - 1)), dma((ITERS, nr - 1)),
             dma((ITERS + 1, nc - 1)), dma((ITERS + 1, nc - 1)),
             dma((ITERS + 1, nr - 1)), dma((ITERS + 1, nr - 1)),
+            dma((ITERS - 1, nc - 1)), dma((ITERS - 1, nc - 1)),
+            dma((ITERS - 1, nr - 1)), dma((ITERS - 1, nr - 1)),
         ],
         compiler_params=pltpu.CompilerParams(
             collective_id=0, has_side_effects=True, vmem_limit_bytes=48 << 20

time: 95.7 us -> 79.3 us (0.83)
  Pallas kernels: 87.8 us -> 71.5 us
    pallas_call x1, Pallas kernels: 87.8 us -> 71.5 us  [shards(): pl.pallas_call(functools.partial(kernel, nr, nc, cb, kb, frames), out_sha...]
where the time goes in v2:
time: 79.3 us; the launch traced here: 79.1 us
  Pallas kernels  71.5 us (90%)
  local copies, waits for them, and re-layouts  4.66 us (6%)
  other arithmetic  2.3 us (3%)
    pallas_call x1, Pallas kernels, shards(): pl.pallas_call(functools.partial(kernel, nr, nc, cb, kb, frames), out_sha...  71.5 us
    unnamed x8, local copies, waits for them, and re-layouts  4.5 us

profile of v2, /device:TPU:0, one launch (start us, length us, event | category | flops | bytes accessed | tf_op | source)
XLA Modules:
  0.0 79.1 jit_solution(3440132676076433801)
XLA Ops:
  0.6 0.7 iota_add_fusion.1
  1.3 0.2 convert_reduce_fusion.1
  1.5 0.1 convert_reduce_fusion.5
  1.6 0.7 iota_add_fusion
  2.3 0.2 convert_reduce_fusion
  2.4 0.1 convert_reduce_fusion.4
  2.6 0.1 convert_reduce_fusion.2
  2.7 0.2 select_reduce_fusion
  2.9 0.1 compare_convert_fusion
  3.0 0.1 concatenate.7.keep
  3.0 0.1 concatenate.6.tab
  3.1 0.0 copy-start
  3.1 1.6 %copy-done = bf16[64,128,128]{2,1,0:T(8,128)(2,1)S(1)} copy-done((bf16[64,128,128]{2,1,0:T(8,128)(2,1)S(1)}, bf16[64,128,128]{2,1,0:T(8,128)(2,1)}, u32[]{:S(2)}) %copy-start) | copy-done | bytes 2097176
  4.7 0.0 copy-start.1
  4.7 0.9 %copy-done.1 = f32[64,512]{1,0:T(8,128)S(1)} copy-done((f32[64,512]{1,0:T(8,128)S(1)}, f32[64,512]{1,0:T(8,128)}, u32[]{:S(2)}) %copy-start.1) | copy-done | bytes 131096
  5.6 0.0 copy-start.2
  5.6 0.7 copy-done.2
  6.3 71.5 %shard_map.68 = (f32[64,512]{1,0:T(8,128)S(1)}, f32[64,512]{1,0:T(8,128)S(1)}) custom-call(s32[288]{0:T(512)S(1)} %concatenate.6.tab, f32[160]{0:T(256)S(1)} %concatenate.7.keep, f32[64,512]{1,0:T(8,128)S(1)} %copy-done.1, f32[1,512]{1,0:T(1,128)S(1)} %bitcast.1, bf16[64,128,128]{2,1,0:T(8,128)(2,1)S(1)} %copy-done), custom_call_target="tpu_custom_call" | custom-call | tf_op jit(solution)/shard_map/pallas_call | solution.py:256
  77.8 0.7 copy.9
  78.4 0.7 copy.10
  (1 shorter events, 0.0 us)
Async XLA Ops:
  3.1 1.6 %copy-start = (bf16[64,128,128]{2,1,0:T(8,128)(2,1)S(1)}, bf16[64,128,128]{2,1,0:T(8,128)(2,1)}, u32[]{:S(2)}) copy-start(bf16[64,128,128]{2,1,0:T(8,128)(2,1)} %blocks_hbm.1) | copy-start | bytes 6291460
  4.7 0.9 %copy-start.1 = (f32[64,512]{1,0:T(8,128)S(1)}, f32[64,512]{1,0:T(8,128)}, u32[]{:S(2)}) copy-start(f32[64,512]{1,0:T(8,128)} %rhs_ref.1) | copy-start | bytes 393220
  5.6 0.7 copy-start.2

commit v3 on v2

--- a/solution.py
+++ b/solution.py
@@ -9,7 +9,8 @@
 
 BLOCK = 128
 ITERS = 2
-UNROLL = 8
+UNROLL = 16
+PARTS = 2
 MESH = pl.DeviceIdType.MESH
 HIGHEST = lax.Precision.HIGHEST
 f32 = jnp.float32
@@ -41,20 +42,28 @@
 
 def kernel(
     nr, nc, cb, kb, frames,
-    tab, keep, rhs_ref, prior_ref, blocks_hbm, sol_ref, res_ref,
-    blocks, panel, foot, sendf, sendb, landf, landb, scan, image, direct, aug,
+    tab_hbm, keep_hbm, rhs_hbm, prior_hbm, blocks_hbm, sol_ref, res_ref,
+    tab, keep, rhs_ref, prior_ref,
+    blocks, panels, feet, sendf, sendb, landf, landb, scan, image, direct, aug,
     gc0, gr0, gc1, gr1, gc2, gr2,
-    blk_sem, ag_s, ag_r, rs_s, rs_r, fg_s, fg_r, br_s, br_r, gc_s, gc_r, gr_s, gr_r,
+    in_sem, blk_sem, ag_s, ag_r, rs_s, rs_r, fg_s, fg_r, br_s, br_r, gc_s, gc_r, gr_s, gr_r,
     nc_s, nc_r, nr_s, nr_r,
 ):
     r = lax.axis_index("row")
     c = lax.axis_index("col")
     nrow, ncol = cb * nc, cb * nr
     half = frames // 2
+    part = frames // PARTS
+    span = lambda h: slice(h * part, (h + 1) * part)
     pending = []
 
-    load = pltpu.make_async_copy(blocks_hbm, blocks, blk_sem)
-    load.start()
+    pairs = ((rhs_hbm, rhs_ref), (prior_hbm, prior_ref), (tab_hbm, tab), (keep_hbm, keep))
+    loads = [
+        pltpu.make_async_copy(src, dst, in_sem.at[i]) for i, (src, dst) in enumerate(pairs)
+    ]
+    loads.append(pltpu.make_async_copy(blocks_hbm, blocks, blk_sem))
+    for load in loads:
+        load.start()
 
     barrier = pltpu.get_barrier_semaphore()
     for axis, me, n in (("row", r, nr), ("col", c, nc)):
@@ -98,13 +107,18 @@
         return jnp.concatenate([packed[:, :frames], packed[:, frames:]], axis=0)
 
     def put_panel(it, value):
-        for b in range(cb):
-            panel[it, r * cb + b] = value[:, b * BLOCK : (b + 1) * BLOCK].astype(bf16)
+        for h in range(PARTS):
+            for b in range(cb):
+                piece = value[span(h), b * BLOCK : (b + 1) * BLOCK]
+                panels[h][it, r * cb + b] = piece.astype(bf16)
 
     def gather_rows(it):
-        return share("row", r, nr, panel.at[it], ag_s.at[it], ag_r.at[it], cb)
-
-    def sweep(source, it, order_at, keep_at, side):
+        return [
+            share("row", r, nr, panels[h].at[it], ag_s.at[it, h], ag_r.at[it, h], cb)
+            for h in range(PARTS)
+        ]
+
+    def sweep(source, it, h, order_at, keep_at, side):
         def body(q, run):
             for u in range(UNROLL):
                 t = q * UNROLL + u
@@ -114,17 +128,18 @@
                     (((1,), (side,)), ((), ())),
                     preferred_element_type=f32,
                 )
-                scan[t] = run
+                scan[h, t] = run
             return run
 
-        lax.fori_loop(0, kb // UNROLL, body, jnp.zeros((frames, BLOCK), f32))
-
-    def segment(end_at, valid_at, i):
-        return scan[tab[end_at + i]] * keep[valid_at + i]
+        lax.fori_loop(0, kb // UNROLL, body, jnp.zeros((part, BLOCK), f32))
+
+    def segment(h, end_at, valid_at, i):
+        return scan[h, tab[end_at + i]] * keep[valid_at + i]
 
     tab_c = 2 * kb + nrow
     keep_c = kb + nrow
 
+    loads[0].wait()
     rhs = rhs_ref[...]
     put_panel(0, rhs)
     fold(gc0, c, pair_gram(rhs, rhs))
@@ -137,56 +152,66 @@
         last = it + 1 == ITERS
         now = rhs_ref if it == 0 else direct
         if it == 0:
-            load.wait()
-        arrive(gather)
-        sweep(panel, it, 0, 0, 1)
-        for i in range(nrow):
-            sendf[it, i] = segment(2 * kb, kb, i).astype(bf16)
-        copies = send(
-            "col", c, nc,
-            lambda p: sendf.at[it, pl.ds(p * cb, cb)], lambda o: landf.at[it, o - 1],
-            rs_s.at[it], rs_r.at[it],
-        )
+            for load in loads[1:]:
+                load.wait()
+        copies = []
+        for h in range(PARTS):
+            arrive(gather[h])
+            sweep(panels[h], it, h, 0, 0, 1)
+            for i in range(nrow):
+                sendf[it, h, i] = segment(h, 2 * kb, kb, i).astype(bf16)
+            copies.append(send(
+                "col", c, nc,
+                lambda p: sendf.at[it, h, pl.ds(p * cb, cb)],
+                lambda o: landf.at[it, h, o - 1],
+                rs_s.at[it, h], rs_r.at[it, h],
+            ))
         if it == 0:
             arrive(gram_cols)
             gr0[r] = total(gc0, nc)
             gram_rows = share("row", r, nr, gr0, gr_s.at[0], gr_r.at[0])
         direction = now[...]
         curvature = pair_gram(direction, prior_ref[...] * direction)
-        arrive(copies)
-        for b in range(cb):
-            own = segment(2 * kb, kb, c * cb + b)
-            for o in range(1, nc):
-                own = own + landf[it, o - 1, b].astype(f32)
-            rounded = own.astype(bf16)
-            foot[it, c * cb + b] = rounded
-            image[:, b * BLOCK : (b + 1) * BLOCK] = own
-        copies = share("col", c, nc, foot.at[it], fg_s.at[it], fg_r.at[it], cb)
-        own = image[...]
-        curvature = curvature + pair_gram(own, own.astype(bf16).astype(f32))
-        fold(gc1.at[it], c, curvature)
-        curve_cols = share("col", c, nc, gc1.at[it], gc_s.at[it + 1], gc_r.at[it + 1])
+        spread = []
+        for h in range(PARTS):
+            arrive(copies[h])
+            for b in range(cb):
+                own = segment(h, 2 * kb, kb, c * cb + b)
+                for o in range(1, nc):
+                    own = own + landf[it, h, o - 1, b].astype(f32)
+                feet[h][it, c * cb + b] = own.astype(bf16)
+                image[span(h), b * BLOCK : (b + 1) * BLOCK] = own
+            if h + 1 == PARTS:
+                own = image[...]
+                curvature = curvature + pair_gram(own, own.astype(bf16).astype(f32))
+                fold(gc1.at[it], c, curvature)
+                curve_cols = share(
+                    "col", c, nc, gc1.at[it], gc_s.at[it + 1], gc_r.at[it + 1]
+                )
+            spread.append(
+                share("col", c, nc, feet[h].at[it], fg_s.at[it, h], fg_r.at[it, h], cb)
+            )
+        copies = []
+        for h in range(PARTS):
+            arrive(spread[h])
+            if h == 0:
+                arrive(curve_cols)
+                gr1[it, r] = total(gc1.at[it], nc)
+                curve_rows = share(
+                    "row", r, nr, gr1.at[it], gr_s.at[it + 1], gr_r.at[it + 1]
+                )
+            sweep(feet[h], it, h, tab_c, keep_c, 0)
+            for i in range(ncol):
+                sendb[it, h, i] = segment(h, tab_c + 2 * kb, keep_c + kb, i).astype(bf16)
+            copies.append(send(
+                "row", r, nr,
+                lambda p: sendb.at[it, h, pl.ds(p * cb, cb)],
+                lambda o: landb.at[it, h, o - 1],
+                br_s.at[it, h], br_r.at[it, h],
+            ))
         if it == 0:
             arrive(gram_rows)
             gram = unfold(total(gr0, nr))
-            aug[:, frames:] = gram
-            eye = lax.broadcasted_iota(jnp.int32, (frames, frames), 0)
-            aug[:, :frames] = (
-                eye == lax.broadcasted_iota(jnp.int32, (frames, frames), 1)
-            ).astype(f32)
-            gram_inverse = gauss_jordan(aug[...], frames)
-        arrive(curve_cols)
-        gr1[it, r] = total(gc1.at[it], nc)
-        curve_rows = share("row", r, nr, gr1.at[it], gr_s.at[it + 1], gr_r.at[it + 1])
-        arrive(copies)
-        sweep(foot, it, tab_c, keep_c, 0)
-        for i in range(ncol):
-            sendb[it, i] = segment(tab_c + 2 * kb, keep_c + kb, i).astype(bf16)
-        copies = send(
-            "row", r, nr,
-            lambda p: sendb.at[it, pl.ds(p * cb, cb)], lambda o: landb.at[it, o - 1],
-            br_s.at[it], br_r.at[it],
-        )
         arrive(curve_rows)
         curvature = unfold(total(gr1.at[it], nr))
         aug[:, :frames] = gram
@@ -194,20 +219,28 @@
         alpha = gauss_jordan(aug[...], frames)
         update = left_t(alpha, direction)
         sol_ref[...] = update if it == 0 else sol_ref[...] + update
-        arrive(copies)
-        for b in range(cb):
-            at = slice(b * BLOCK, (b + 1) * BLOCK)
-            own = segment(tab_c + 2 * kb, keep_c + kb, r * cb + b)
-            for o in range(1, nr):
-                own = own + landb[it, o - 1, b].astype(f32)
-            image[:, at] = own + prior_ref[:, at] * now[:, at]
+        for h in range(PARTS):
+            arrive(copies[h])
+            for b in range(cb):
+                at = slice(b * BLOCK, (b + 1) * BLOCK)
+                own = segment(h, tab_c + 2 * kb, keep_c + kb, r * cb + b)
+                for o in range(1, nr):
+                    own = own + landb[it, h, o - 1, b].astype(f32)
+                image[span(h), at] = own + prior_ref[:, at] * now[span(h), at]
         residual = (rhs_ref if it == 0 else res_ref)[...] - left_t(alpha, image[...])
         res_ref[...] = residual
         if not last:
             fold(gc2.at[it], c, pair_gram(residual, residual))
             arrive(share("col", c, nc, gc2.at[it], nc_s.at[it], nc_r.at[it]))
             gr2[it, r] = total(gc2.at[it], nc)
-            arrive(share("row", r, nr, gr2.at[it], nr_s.at[it], nr_r.at[it]))
+            gram_rows = share("row", r, nr, gr2.at[it], nr_s.at[it], nr_r.at[it])
+            aug[:, frames:] = gram
+            eye = lax.broadcasted_iota(jnp.int32, (frames, frames), 0)
+            aug[:, :frames] = (
+                eye == lax.broadcasted_iota(jnp.int32, (frames, frames), 1)
+            ).astype(f32)
+            gram_inverse = gauss_jordan(aug[...], frames)
+            arrive(gram_rows)
             gram = unfold(total(gr2.at[it], nr))
             beta = dot(gram_inverse, gram, ((1,), (0,)))
             direct[...] = residual + left_t(beta, direction)
@@ -247,26 +280,30 @@
     tab = jnp.concatenate(ints_r + ints_c)
     keep = jnp.concatenate(keep_r + keep_c)
     vm = pl.BlockSpec(memory_space=pltpu.VMEM)
-    sm = pl.BlockSpec(memory_space=pltpu.SMEM)
     dma = pltpu.SemaphoreType.DMA
-    tile = (frames, BLOCK)
+    tile = (frames // PARTS, BLOCK)
+    pieces = (ITERS, PARTS)
     half = (frames // 2, 2 * frames)
     wide = (frames, 2 * frames)
     out = jax.ShapeDtypeStruct(right_side.shape, f32)
     return pl.pallas_call(
         functools.partial(kernel, nr, nc, cb, kb, frames),
         out_shape=(out, out),
-        in_specs=[sm, sm, vm, vm, pl.BlockSpec(memory_space=pl.ANY)],
+        in_specs=[pl.BlockSpec(memory_space=pl.ANY)] * 5,
         out_specs=(vm, vm),
         scratch_shapes=[
+            pltpu.SMEM(tab.shape, jnp.int32),
+            pltpu.SMEM(keep.shape, f32),
+            pltpu.VMEM(right_side.shape, f32),
+            pltpu.VMEM((1, pix), f32),
             pltpu.VMEM(blocks.shape, bf16),
-            pltpu.VMEM((ITERS, ncol) + tile, bf16),
-            pltpu.VMEM((ITERS, nrow) + tile, bf16),
-            pltpu.VMEM((ITERS, nrow) + tile, bf16),
-            pltpu.VMEM((ITERS, ncol) + tile, bf16),
-            pltpu.VMEM((ITERS, nc - 1, cb) + tile, bf16),
-            pltpu.VMEM((ITERS, nr - 1, cb) + tile, bf16),
-            pltpu.VMEM((kb,) + tile, f32),
+            [pltpu.VMEM((ITERS, ncol) + tile, bf16)] * PARTS,
+            [pltpu.VMEM((ITERS, nrow) + tile, bf16)] * PARTS,
+            pltpu.VMEM(pieces + (nrow,) + tile, bf16),
+            pltpu.VMEM(pieces + (ncol,) + tile, bf16),
+            pltpu.VMEM(pieces + (nc - 1, cb) + tile, bf16),
+            pltpu.VMEM(pieces + (nr - 1, cb) + tile, bf16),
+            pltpu.VMEM((PARTS, kb) + tile, f32),
             pltpu.VMEM(right_side.shape, f32),
             pltpu.VMEM(right_side.shape, f32),
             pltpu.VMEM(wide, f32),
@@ -276,11 +313,12 @@
             pltpu.VMEM((ITERS, nr) + half, f32),
             pltpu.VMEM((ITERS - 1, nc) + half, f32),
             pltpu.VMEM((ITERS - 1, nr) + half, f32),
+            dma((4,)),
             dma,
-            dma((ITERS, nr - 1)), dma((ITERS, nr - 1)),
-            dma((ITERS, nc - 1)), dma((ITERS, nc - 1)),
-            dma((ITERS, nc - 1)), dma((ITERS, nc - 1)),
-            dma((ITERS, nr - 1)), dma((ITERS, nr - 1)),
+            dma(pieces + (nr - 1,)), dma(pieces + (nr - 1,)),
+            dma(pieces + (nc - 1,)), dma(pieces + (nc - 1,)),
+            dma(pieces + (nc - 1,)), dma(pieces + (nc - 1,)),
+            dma(pieces + (nr - 1,)), dma(pieces + (nr - 1,)),
             dma((ITERS + 1, nc - 1)), dma((ITERS + 1, nc - 1)),
             dma((ITERS + 1, nr - 1)), dma((ITERS + 1, nr - 1)),
             dma((ITERS - 1, nc - 1)), dma((ITERS - 1, nc - 1)),

time: 79.3 us -> 75.4 us (0.951)
  Pallas kernels: 71.5 us -> 67.5 us
    pallas_call x1, Pallas kernels: 71.5 us -> 67.5 us  [shards(): pl.pallas_call(functools.partial(kernel, nr, nc, cb, kb, frames), out_sha...]
where the time goes in v3:
time: 75.4 us; the launch traced here: 75.1 us
  Pallas kernels  67.5 us (90%)
  local copies, waits for them, and re-layouts  4.66 us (6%)
  other arithmetic  2.3 us (3%)
    pallas_call x1, Pallas kernels, shards(): pl.pallas_call(functools.partial(kernel, nr, nc, cb, kb, frames), out_sha...  67.5 us
    unnamed x8, local copies, waits for them, and re-layouts  4.5 us

profile of v3, /device:TPU:0, one launch (start us, length us, event | category | flops | bytes accessed | tf_op | source)
XLA Modules:
  0.0 75.1 jit_solution(4919630586769100741)
XLA Ops:
  0.6 0.7 iota_add_fusion.1
  1.3 0.2 convert_reduce_fusion.1
  1.5 0.1 convert_reduce_fusion.5
  1.6 0.7 iota_add_fusion
  2.3 0.2 convert_reduce_fusion
  2.4 0.1 convert_reduce_fusion.4
  2.6 0.1 convert_reduce_fusion.2
  2.7 0.2 select_reduce_fusion
  2.9 0.1 compare_convert_fusion
  3.0 0.1 concatenate.7.keep_hbm
  3.0 0.1 concatenate.6.tab_hbm
  3.1 0.0 copy-start
  3.1 1.6 %copy-done = bf16[64,128,128]{2,1,0:T(8,128)(2,1)S(1)} copy-done((bf16[64,128,128]{2,1,0:T(8,128)(2,1)S(1)}, bf16[64,128,128]{2,1,0:T(8,128)(2,1)}, u32[]{:S(2)}) %copy-start) | copy-done | bytes 2097176
  4.7 0.0 copy-start.1
  4.7 0.9 %copy-done.1 = f32[64,512]{1,0:T(8,128)S(1)} copy-done((f32[64,512]{1,0:T(8,128)S(1)}, f32[64,512]{1,0:T(8,128)}, u32[]{:S(2)}) %copy-start.1) | copy-done | bytes 131096
  5.6 0.0 copy-start.2
  5.6 0.7 copy-done.2
  6.3 67.5 %shard_map.68 = (f32[64,512]{1,0:T(8,128)S(1)}, f32[64,512]{1,0:T(8,128)S(1)}) custom-call(s32[288]{0:T(512)S(1)} %concatenate.6.tab_hbm, f32[160]{0:T(256)S(1)} %concatenate.7.keep_hbm, f32[64,512]{1,0:T(8,128)S(1)} %copy-done.1, f32[1,512]{1,0:T(1,128)S(1)} %bitcast.1, bf16[64,128,128]{2,1,0:T(8,128)(2,1)S(1)} %copy-done), custom_call_target="tpu_custom_call" | custom-call | tf_op jit(solution)/shard_map/pallas_call | solution.py:289
  73.8 0.7 copy.9
  74.5 0.7 copy.10
  (1 shorter events, 0.0 us)
Async XLA Ops:
  3.1 1.6 %copy-start = (bf16[64,128,128]{2,1,0:T(8,128)(2,1)S(1)}, bf16[64,128,128]{2,1,0:T(8,128)(2,1)}, u32[]{:S(2)}) copy-start(bf16[64,128,128]{2,1,0:T(8,128)(2,1)} %blocks_hbm.1) | copy-start | bytes 6291460
  4.7 0.9 %copy-start.1 = (f32[64,512]{1,0:T(8,128)S(1)}, f32[64,512]{1,0:T(8,128)}, u32[]{:S(2)}) copy-start(f32[64,512]{1,0:T(8,128)} %rhs_hbm.1) | copy-start | bytes 393220
  5.6 0.7 copy-start.2
